TPU v7x, 32 devices: a whole 2x2x4 slice. The times are simulated.
32 devices in a mesh: alpha: 4 (over y, core), beta: 8 (over z, x).
Axes of the slice: x: 2, y: 2, z: 4, core: 2. Of those that a mesh axis runs over, the one named last changes fastest.
Arguments:
- coeffs: float32 [8, 1024], P('alpha', 'beta'), may hold values from -6 to 6
- alpha_target: int32 [8, 132], P('alpha'), may hold values from 0 to 7
- alpha_pair: int32 [8, 132], P('alpha'), may hold values from 0 to 483
- alpha_sign: int32 [8, 132], P('alpha'), may hold values from -1 to 1
- beta_target: int32 [1024, 132], P('beta'), may hold values from 0 to 1023
- beta_pair: int32 [1024, 132], P('beta'), may hold values from 0 to 483
- beta_sign: int32 [1024, 132], P('beta'), may hold values from -1 to 1
- integrals: float32 [484, 484], replicated
- one_body: float32 [22, 22], replicated
Outputs:
- sigma: float32 [8, 1024], P('alpha', 'beta')
All inputs are finite; a program needn't handle non-finite values.
Results may differ from a plain program's by a relative error of at most 0.0003.
Values sent between devices are 32-bit elements; how exact they have to be, the bound alone decides.
A program may use at most 64 MiB of HBM per device.

v0:
```python
import jax
import jax.numpy as jnp
from jax import lax
from jax.sharding import PartitionSpec as P

ROWB = 1


def per_device(
    coeffs,
    alpha_target,
    alpha_pair,
    alpha_sign,
    beta_target,
    beta_pair,
    beta_sign,
    integrals,
    one_body,
):
    highest = lax.Precision.HIGHEST
    rows_alpha, cols_beta = coeffs.shape
    slot_count = alpha_target.shape[1]
    norbit = one_body.shape[0]
    npairs = norbit * norbit
    beta_total = cols_beta * lax.axis_size("beta")
    h_flat = one_body.reshape(npairs)
    pair_ids = jnp.arange(npairs, dtype=jnp.int32)
    swapped = beta_pair % norbit * norbit + beta_pair // norbit
    beta_phase = beta_sign.astype(jnp.float32)
    flat_target = beta_target.reshape(cols_beta * slot_count)
    column_slab = lax.all_gather(coeffs, "alpha", axis=0, tiled=True)
    gathered = column_slab[alpha_target]
    local_parts = []
    spread_parts = []
    for block in range(rows_alpha // ROWB):
        lower = block * ROWB
        pairs = alpha_pair[lower : lower + ROWB]
        signs = alpha_sign[lower : lower + ROWB].astype(jnp.float32)
        picks = (pairs[:, :, None] == pair_ids[None, None, :]).astype(jnp.float32) * signs[
            :, :, None
        ]
        dens = jnp.einsum("isp,isb->ipb", picks, gathered[lower : lower + ROWB], precision=highest)
        c_rows = coeffs[lower : lower + ROWB]
        fock = (
            jnp.einsum("pq,ipb->iqb", integrals, dens, precision=highest)
            + h_flat[None, :, None] * c_rows[:, None, :]
        )
        local = jnp.einsum("p,ipb->ib", h_flat, dens, precision=highest)
        fock_cols = jnp.transpose(fock, (2, 1, 0))
        values = (
            jnp.take_along_axis(fock_cols, swapped[:, :, None], axis=1) * beta_phase[:, :, None]
        )
        spread = jax.ops.segment_sum(
            values.reshape(cols_beta * slot_count, ROWB), flat_target, num_segments=beta_total
        )
        local_parts.append(local)
        spread_parts.append(spread.T)
    summed = lax.psum_scatter(
        jnp.concatenate(spread_parts, axis=0), "beta", scatter_dimension=1, tiled=True
    )
    return jnp.concatenate(local_parts, axis=0) + summed


def solution(mesh):
    placed = (
        P("alpha", "beta"),
        P("alpha", None),
        P("alpha", None),
        P("alpha", None),
        P("beta", None),
        P("beta", None),
        P("beta", None),
        P(),
        P(),
    )
    return jax.shard_map(
        per_device, mesh=mesh, in_specs=placed, out_specs=P("alpha", "beta"), check_vma=False
    )
```

profile of v0, /device:TPU:0, one launch (start us, length us, event | category | flops | bytes accessed | tf_op | source)
XLA Modules:
  0.0 551.8 jit_solution(2553725765282024006)
XLA Ops:
  6.5 0.0 copy-start
  6.5 0.0 reduce-scatter.4.cloned.1.call-start
  6.5 0.8 slice_bitcast_fusion
  7.3 0.8 reshape.330
  8.1 0.7 compare_select_fusion.3
  8.8 0.1 reshape.352
  8.9 0.8 fusion.20
  9.7 0.8 slice_convert_fusion
  10.4 6.3 %all-gather = f32[4,2,128]{2,1,0:T(2,128)S(1)} all-gather(f32[1,2,128]{2,1,0:T(2,128)} %bitcast.81), channel_id=1, replica_groups=mesh['alpha'=4,'beta'=8] {'alpha'}, dimensions={0}, use_global_device_ids=true | all-gather | bytes 5120 | tf_op jit(solution)/shard_map/all_gather | solution.py:31
  16.7 1.0 copy.16
  17.7 1.0 copy.19
  18.7 0.2 shift-left_or_fusion
  18.9 0.1 reshape.395
  19.0 1.0 copy.15
  20.0 0.1 reshape.362
  20.2 1.0 gather_fusion
  21.2 0.3 compare_select_fusion.1
  21.6 1.0 fusion.7
  22.6 0.0 copy-done
  22.6 1.8 fusion.1
  24.4 107.8 %gather_fusion.1 = f32[16896]{0:T(1024)S(1)} fusion(f32[128,484]{0,1:T(8,128)S(1)} %fusion.1, s32[16896]{0:T(1024)S(1)} %reshape.395), kind=kCustom, calls=%fused_computation.clone | custom fusion | bytes 270336 | tf_op jit(solution)/shard_map/jit(take_along_axis)/gather | solution.py:51
  132.2 0.2 reshape.398
  132.4 0.2 bitcast_multiply_fusion.1
  132.6 0.1 reshape.364
  132.7 0.3 compare_select_fusion
  133.1 1.0 fusion.4
  134.1 1.8 fusion.3
  135.8 107.8 %gather_fusion.2 = f32[16896]{0:T(1024)S(1)} fusion(f32[128,484]{0,1:T(8,128)S(1)} %fusion.3, s32[16896]{0:T(1024)S(1)} %reshape.395), kind=kCustom, calls=%fused_computation.1.clone | custom fusion | bytes 270336 | tf_op jit(solution)/shard_map/jit(take_along_axis)/gather | solution.py:51
  243.7 0.0 copy-start.1
  243.7 0.2 reshape.403
  243.9 0.1 reshape.374
  244.0 117.0 %scatter_custom_fusion = f32[1024]{0:T(1024)S(1)} fusion(s32[16896]{0:T(1024)S(1)} %reshape.362, f32[16896]{0:T(1024)S(1)} %reshape.364, f32[]{:T(128)} %constant.31.clone.1), kind=kCustom, calls=%fused_computation.39 | custom fusion | flops 16896 | bytes 4100 | tf_op jit(solution)/shard_map/scatter-add | solution.py:53
  361.0 117.0 %scatter_custom_fusion.1 = f32[1024]{0:T(1024)S(1)} fusion(s32[16896]{0:T(1024)S(1)} %reshape.362, f32[16896]{0:T(1024)S(1)} %reshape.374, f32[]{:T(128)} %constant.31.clone.1), kind=kCustom, calls=%fused_computation.37 | custom fusion | flops 16896 | bytes 4100 | tf_op jit(solution)/shard_map/scatter-add | solution.py:53
  478.0 1.0 copy.20
  479.0 0.0 reduce-scatter.4.cloned.1.call-update
  479.0 0.0 copy-done.1
  479.0 0.1 reshape.404
  479.1 0.3 fusion.21
  479.4 0.3 fusion.22
  479.7 63.7 %reduce-scatter.4.cloned.1.call-done = f32[128,2]{1,0:T(8,128)} async-done(((f32[1024,2]{1,0:T(8,128)}), f32[128,2]{1,0:T(8,128)}) %reduce-scatter.4.cloned.1.call-update) | async-done | bytes 1040
  543.4 0.9 copy.21
  544.3 0.6 maximum_add_fusion
  (3 shorter events, 0.0 us)
Async XLA Ops:
  6.5 16.0 %copy-start = (f32[484,484]{1,0:T(8,128)S(1)}, f32[484,484]{1,0:T(8,128)}, u32[]{:S(2)}) copy-start(f32[484,484]{1,0:T(8,128)} %param.18) | copy-start | bytes 2811076
  6.5 536.9 %reduce-scatter.4.cloned.1.call-start = ((), (), s32[]{:S(2)}) async-start(), calls=%async_computation.1 | async-start | bytes 589824
  243.7 235.4 %copy-start.1 = (f32[22,22]{1,0:T(8,128)S(1)}, f32[22,22]{1,0:T(8,128)}, u32[]{:S(2)}) copy-start(f32[22,22]{1,0:T(8,128)} %param.19) | copy-start | bytes 5812
Sparse Core Ops, SparseCore 0:
  479.2 64.2 reduce-scatter.3
where the time goes:
time: 552 us
  other arithmetic  237 us (43%)
  local copies, waits for them, and re-layouts  225 us (41%)
  waiting for transfers between devices  63.7 us (12%)
  between operations  13.6 us (2%)
  blocking collectives  6.3 us (1%)
  matrix products  6.14 us (1%)
    scatter-add x2, other arithmetic, per_device(): jax.ops.segment_sum(values.reshape(cols_beta * slot_count, ROWB), flat_ta...  234 us
    gather x5, local copies, waits for them, and re-layouts, per_device(): jnp.take_along_axis(fock_cols, swapped[:, :, None], axis=1)  216 us
    unnamed x2, waiting for transfers between devices  63.7 us
  transfers between devices with their start and end apart: 1, of which 1 were waited for; matrix products, arithmetic and copies ran while one was open for 0% of the time, Pallas kernels for 0%

commit v1 on v0

v1 whole, which is shorter than its diff:
```python
import functools

import jax
import jax.numpy as jnp
from jax import lax
from jax.experimental import pallas as pl
from jax.experimental.pallas import tpu as pltpu
from jax.sharding import PartitionSpec as P

MESH = pl.DeviceIdType.MESH
LANES = 128
NT = (((1,), (1,)), ((), ()))
NN = (((1,), (0,)), ((), ()))


def dot(a, b, dims=NN):
    return lax.dot_general(a, b, dims, preferred_element_type=jnp.float32)


def split(x):
    top = x.astype(jnp.bfloat16).astype(jnp.float32)
    return top, x - top


def divider(n, limit):
    s = 16
    m = (1 << s) // n + 1
    assert all((x * m) >> s == x // n for x in range(limit)) and limit * m < 2**31
    return m, s


def lane_pick(table, lane, chunk):
    out = None
    for i in range(table.shape[1] // LANES):
        part = jnp.take_along_axis(
            table[:, i * LANES : (i + 1) * LANES], lane, axis=1, mode="promise_in_bounds"
        )
        out = part if out is None else jnp.where(chunk == i, part, out)
    return out


def kernel(
    na,
    nb,
    step_rows,
    coeffs,
    a_target,
    a_pair,
    a_sign,
    b_target,
    b_pair,
    b_sign,
    integrals,
    one_body,
    out,
    at_v,
    ap_v,
    as_v,
    bt_v,
    bp_v,
    bs_v,
    int_v,
    ob_v,
    slab,
    g_v,
    owner_v,
    lo_v,
    vals,
    hot,
    send,
    recv,
    load_sem,
    ag_send,
    ag_recv,
    rs_send,
    rs_recv,
):
    rows, cols = coeffs.shape
    slots = a_target.shape[1]
    norb = one_body.shape[0]
    npairs = norb * norb
    wide = g_v.shape[1]
    alphas = na * rows
    me_a = lax.axis_index("alpha")
    me_b = lax.axis_index("beta")
    f32, bf16 = jnp.float32, jnp.bfloat16

    loads = [
        pltpu.make_async_copy(src, dst, load_sem.at[i])
        for i, (src, dst) in enumerate(
            (
                (a_target, at_v),
                (a_pair, ap_v),
                (a_sign, as_v),
                (one_body, ob_v),
                (integrals, int_v),
                (b_target, bt_v),
                (b_pair, bp_v),
                (b_sign, bs_v),
            )
        )
    ]
    for load in loads:
        load.start()
    barrier = pltpu.get_barrier_semaphore()
    for k in range(1, na):
        pl.semaphore_signal(barrier, inc=1, device_id=(lax.rem(me_a + k, na), me_b), device_id_type=MESH)
    for k in range(1, nb):
        pl.semaphore_signal(barrier, inc=1, device_id=(me_a, lax.rem(me_b + k, nb)), device_id_type=MESH)
    pl.semaphore_wait(barrier, na + nb - 2)

    gathers = []
    for k in range(1, na):
        copy = pltpu.make_async_remote_copy(
            src_ref=coeffs,
            dst_ref=slab.at[me_a],
            send_sem=ag_send.at[k],
            recv_sem=ag_recv.at[k],
            device_id=(lax.rem(me_a + k, na), me_b),
            device_id_type=MESH,
        )
        copy.start()
        gathers.append(copy)

    for i in range(5):
        loads[i].wait()
    pair_ids = lax.broadcasted_iota(jnp.int32, (wide, slots), 0)
    string_ids = lax.broadcasted_iota(jnp.int32, (alphas, slots), 0)
    counts = []
    for a in range(rows):
        hits = jnp.where(pair_ids == ap_v[a : a + 1, :], 1.0, 0.0).astype(bf16)
        reach = jnp.where(string_ids == at_v[a : a + 1, :], as_v[a : a + 1, :].astype(f32), 0.0)
        counts.append(dot(reach.astype(bf16), hits, NT))
    counts = jnp.concatenate(counts, axis=0)
    mul, shift = divider(norb, wide)
    q = lax.broadcasted_iota(jnp.int32, (norb, wide), 1)
    q_row = (q * mul) >> shift
    q_col = q - q_row * norb
    orbital = lax.broadcasted_iota(jnp.int32, (norb, wide), 0)
    spread_h = lax.dot_general(
        ob_v[...],
        jnp.where(q_col == orbital, 1.0, 0.0),
        NN,
        precision=lax.Precision.HIGHEST,
        preferred_element_type=f32,
    )
    h = jnp.sum(jnp.where(q_row == orbital, spread_h, 0.0), axis=0, keepdims=True)
    weight = jnp.sum(counts * h, axis=1, keepdims=True)
    exact = counts[:, :npairs].astype(bf16)
    int_top, int_rest = split(int_v[...])
    g_v[...] = jnp.zeros_like(g_v)
    g_v[:, :npairs] = dot(exact, int_top.astype(bf16)) + dot(exact, int_rest.astype(bf16))
    line = lax.broadcasted_iota(jnp.int32, (rows * alphas, wide), 0)
    own = line == me_a * rows
    for a in range(1, rows):
        own = own | (line == a * alphas + me_a * rows + a)
    g = g_v[...] + jnp.where(own, h, 0.0)

    full, rem = slots // LANES, slots % LANES
    loads[5].wait()
    bits = cols.bit_length() - 1

    def to_rows(ref, values):
        for i in range(full):
            ref[i * cols : (i + 1) * cols, :] = values[i]
        if rem:
            ref[full * cols : full * cols + rem, :] = values[full].T[:rem, :]

    def chunks(ref):
        parts = [ref[:, i * LANES : (i + 1) * LANES] for i in range(full)]
        if rem:
            last = ref[:, full * LANES :]
            parts.append(jnp.concatenate([last, jnp.zeros((cols, LANES - rem), last.dtype)], axis=1))
        return parts

    targets = [t.astype(f32) for t in chunks(bt_v)]
    targets = [jnp.floor(t * (1.0 / cols)) for t in targets], targets
    to_rows(owner_v, targets[0])
    to_rows(lo_v, [t - o * cols for o, t in zip(*targets)])
    lo_ids = lax.broadcasted_iota(jnp.int32, (cols, LANES), 0).astype(f32)
    items = slots * cols // LANES

    @pl.loop(0, items // step_rows)
    def _(i):
        for r in range(step_rows):
            row = i * step_rows + r
            match = lo_ids == lo_v[pl.ds(row, 1), :]
            hot[:, pl.ds(pl.multiple_of(row * LANES, LANES), LANES)] = jnp.where(match, 1.0, 0.0).astype(bf16)

    loads[6].wait()
    loads[7].wait()
    lanes, pieces, signs = [], [], []
    for p, s in zip(chunks(bp_v), chunks(bs_v)):
        k = (p * mul) >> shift
        swapped = (p - k * norb) * norb + k
        lanes.append(swapped & (LANES - 1))
        pieces.append(swapped >> (LANES.bit_length() - 1))
        signs.append(s.astype(f32))

    for copy in gathers:
        copy.wait()
    slab[me_a] = coeffs[...]
    c = jnp.concatenate([slab[i] for i in range(na)], axis=0)
    c_top, c_rest = split(c)
    lhs = jnp.concatenate([c_top, c_rest, c_top], axis=0).T.astype(bf16)
    local = []
    for a in range(rows):
        local.append(jnp.sum(weight[a * alphas : (a + 1) * alphas] * c, axis=0, keepdims=True))
        g_top, g_rest = split(g[a * alphas : (a + 1) * alphas])
        fock = dot(lhs, jnp.concatenate([g_top, g_top, g_rest], axis=0).astype(bf16))
        picked = [lane_pick(fock, l, p) * s for l, p, s in zip(lanes, pieces, signs)]
        parts = [split(v) for v in picked]
        to_rows(vals.at[a], [v[0] for v in parts])
        to_rows(vals.at[rows + a], [v[1] for v in parts])

    owner_ids = lax.broadcasted_iota(jnp.int32, (nb, LANES), 0).astype(f32)

    def step(i, total):
        lhs = []
        for r in range(step_rows):
            row = i * step_rows + r
            match = owner_ids == owner_v[pl.ds(row, 1), :]
            lhs.append(
                jnp.concatenate([jnp.where(match, vals[m, pl.ds(row, 1), :], 0.0) for m in range(2 * rows)], axis=0)
            )
        lhs = jnp.concatenate(lhs, axis=1).astype(bf16)
        width = step_rows * LANES
        return total + dot(lhs, hot[:, pl.ds(pl.multiple_of(i * width, LANES), width)], NT)

    total = lax.fori_loop(0, items // step_rows, step, jnp.zeros((2 * rows * nb, cols), f32))
    for a in range(rows):
        send[:, a, :] = total[a * nb : (a + 1) * nb] + total[(rows + a) * nb : (rows + a + 1) * nb]

    copies = []
    for k in range(1, nb):
        to = lax.rem(me_b + k, nb)
        copy = pltpu.make_async_remote_copy(
            src_ref=send.at[to],
            dst_ref=recv.at[k],
            send_sem=rs_send.at[k],
            recv_sem=rs_recv.at[k],
            device_id=(me_a, to),
            device_id_type=MESH,
        )
        copy.start()
        copies.append(copy)
    result = jnp.concatenate(local, axis=0) + send[me_b]
    for copy in copies:
        copy.wait()
    for k in range(1, nb):
        result = result + recv[k]
    out[...] = result


def solution(mesh):
    na, nb = mesh.shape["alpha"], mesh.shape["beta"]

    def per_device(coeffs, a_target, a_pair, a_sign, b_target, b_pair, b_sign, integrals, one_body):
        rows, cols = coeffs.shape
        slots = a_target.shape[1]
        norb = one_body.shape[0]
        wide = pl.cdiv(norb * norb, LANES) * LANES
        items = slots * cols // LANES
        step_rows = next(n for n in (6, 4, 3, 2, 1) if items % n == 0)
        i32, f32 = jnp.int32, jnp.float32
        padded = pl.cdiv(items, 8) * 8
        return pl.pallas_call(
            functools.partial(kernel, na, nb, step_rows),
            out_shape=jax.ShapeDtypeStruct((rows, cols), f32),
            in_specs=[pl.BlockSpec(memory_space=pltpu.VMEM)] + [pl.BlockSpec(memory_space=pl.ANY)] * 8,
            out_specs=pl.BlockSpec(memory_space=pltpu.VMEM),
            scratch_shapes=[
                pltpu.VMEM(a_target.shape, i32),
                pltpu.VMEM(a_pair.shape, i32),
                pltpu.VMEM(a_sign.shape, i32),
                pltpu.VMEM(b_target.shape, i32),
                pltpu.VMEM(b_pair.shape, i32),
                pltpu.VMEM(b_sign.shape, i32),
                pltpu.VMEM(integrals.shape, f32),
                pltpu.VMEM(one_body.shape, f32),
                pltpu.VMEM((na, rows, cols), f32),
                pltpu.VMEM((rows * na * rows, wide), f32),
                pltpu.VMEM((padded, LANES), f32),
                pltpu.VMEM((padded, LANES), f32),
                pltpu.VMEM((2 * rows, padded, LANES), f32),
                pltpu.VMEM((cols, items * LANES), jnp.bfloat16),
                pltpu.VMEM((nb, rows, cols), f32),
                pltpu.VMEM((nb, rows, cols), f32),
                pltpu.SemaphoreType.DMA((8,)),
                pltpu.SemaphoreType.DMA((na,)),
                pltpu.SemaphoreType.DMA((na,)),
                pltpu.SemaphoreType.DMA((nb,)),
                pltpu.SemaphoreType.DMA((nb,)),
            ],
            compiler_params=pltpu.CompilerParams(collective_id=0, has_side_effects=True),
        )(coeffs, a_target, a_pair, a_sign, b_target, b_pair, b_sign, integrals, one_body)

    placed = (
        P("alpha", "beta"),
        P("alpha", None),
        P("alpha", None),
        P("alpha", None),
        P("beta", None),
        P("beta", None),
        P("beta", None),
        P(),
        P(),
    )
    return jax.shard_map(
        per_device, mesh=mesh, in_specs=placed, out_specs=P("alpha", "beta"), check_vma=False
    )
```

time: 552 us -> 22.9 us (0.04)
  other arithmetic: 237 us -> 0 us
  local copies, waits for them, and re-layouts: 225 us -> 4.53 us
  waiting for transfers between devices: 63.7 us -> 0 us
  Pallas kernels: 0 us -> 18.1 us
  between operations: 13.6 us -> 0.01 us
  blocking collectives: 6.3 us -> 0 us
  matrix products: 6.14 us -> 0 us
    scatter-add x2 -> x0, other arithmetic: 234 us -> none  [per_device(): jax.ops.segment_sum(values.reshape(cols_beta * slot_count, ROWB), flat_ta...]
    gather x6 -> x0, local copies, waits for them, and re-layouts: 217 us -> none  [the longest x5 216 us: per_device(): jnp.take_along_axis(fock_cols, swapped[:, :, None], axis=1)]
    unnamed x2 -> x0, waiting for transfers between devices: 63.7 us -> none
    pallas_call x0 -> x1, Pallas kernels: none -> 18.1 us  [per_device(): pl.pallas_call(functools.partial(kernel, na, nb, step_rows), out_shape=ja...]
    all_gather x1 -> x0, blocking collectives: 6.3 us -> none  [per_device(): column_slab = lax.all_gather(coeffs, 'alpha', axis=0, tiled=True)]
    dot_general x6 -> x0, matrix products: 6.14 us -> none  [the longest x2 3.59 us: per_device(): jnp.einsum('pq,ipb->iqb', integrals, dens, precision=highest)]
  transfers between devices with their start and end apart: 1 -> 0, of which waited for: 1 -> 0; matrix products, arithmetic and copies ran while one was open for 0% -> 0% of each run, Pallas kernels for 0% -> 0%
where the time goes in v1:
time: 22.9 us; the launch traced here: 22.7 us
  Pallas kernels  18.1 us (79%)
  local copies, waits for them, and re-layouts  4.53 us (20%)
    pallas_call x1, Pallas kernels, per_device(): pl.pallas_call(functools.partial(kernel, na, nb, step_rows), out_shape=ja...  18.1 us
    unnamed x8, local copies, waits for them, and re-layouts  4.53 us

profile of v1, /device:TPU:0, one launch (start us, length us, event | category | flops | bytes accessed | tf_op | source)
XLA Modules:
  0.0 22.7 jit_solution(13712824374713191030)
XLA Ops:
  0.0 0.0 copy-start
  0.0 1.6 %copy.10.b_target = s32[128,132]{1,0:T(8,128)} copy(s32[128,132]{0,1:T(8,128)} %param.13) | data formatting | bytes 135168 | tf_op args[4]
  1.7 0.0 copy-done
  1.7 0.0 copy-start.1
  1.7 0.7 %copy.11.b_pair = s32[128,132]{1,0:T(8,128)} copy(s32[128,132]{0,1:T(8,128)S(1)} %copy-done) | data formatting | bytes 135168 | tf_op args[5]
  2.4 0.1 copy-done.1
  2.5 0.8 %copy.12.b_sign = s32[128,132]{1,0:T(8,128)} copy(s32[128,132]{0,1:T(8,128)S(1)} %copy-done.1) | data formatting | bytes 135168 | tf_op args[6]
  3.3 18.1 %shard_map.91 = f32[2,128]{1,0:T(2,128)} custom-call(f32[2,128]{1,0:T(2,128)} %coeffs.1, s32[2,132]{1,0:T(2,128)} %a_target.1, s32[2,132]{1,0:T(2,128)} %a_pair.1, s32[2,132]{1,0:T(2,128)} %a_sign.1, s32[128,132]{1,0:T(8,128)} %copy.10.b_target, s32[128,132]{1,0:T(8,128)} %copy.11.b_pair, s32[128,132]{1,0:T(8,128)} %copy.12.b_sign, f32[484,484]{1,0:T(8,128)} %integrals.1, ...), custom_call_target="tpu_custom_call" | custom-call | tf_op jit(solution)/shard_map/pallas_call | solution.py:267
  21.4 1.2 %copy.14 = f32[2,128]{1,0:T(2,128)} copy(f32[2,128]{1,0:T(2,128)} %shard_map.91) | data formatting | bytes 2048
Async XLA Ops:
  0.0 1.7 %copy-start = (s32[128,132]{0,1:T(8,128)S(1)}, s32[128,132]{0,1:T(8,128)}, u32[]{:S(2)}) copy-start(s32[128,132]{0,1:T(8,128)} %param.14) | copy-start | bytes 202756
  1.7 0.9 %copy-start.1 = (s32[128,132]{0,1:T(8,128)S(1)}, s32[128,132]{0,1:T(8,128)}, u32[]{:S(2)}) copy-start(s32[128,132]{0,1:T(8,128)} %param.15) | copy-start | bytes 202756

commit v2 on v1

--- a/solution.py
+++ b/solution.py
@@ -42,6 +42,7 @@
 def kernel(
     na,
     nb,
+    build_rows,
     step_rows,
     coeffs,
     a_target,
@@ -53,6 +54,7 @@
     integrals,
     one_body,
     out,
+    c_v,
     at_v,
     ap_v,
     as_v,
@@ -89,6 +91,7 @@
         pltpu.make_async_copy(src, dst, load_sem.at[i])
         for i, (src, dst) in enumerate(
             (
+                (coeffs, c_v),
                 (a_target, at_v),
                 (a_pair, ap_v),
                 (a_sign, as_v),
@@ -107,22 +110,7 @@
         pl.semaphore_signal(barrier, inc=1, device_id=(lax.rem(me_a + k, na), me_b), device_id_type=MESH)
     for k in range(1, nb):
         pl.semaphore_signal(barrier, inc=1, device_id=(me_a, lax.rem(me_b + k, nb)), device_id_type=MESH)
-    pl.semaphore_wait(barrier, na + nb - 2)
-
-    gathers = []
-    for k in range(1, na):
-        copy = pltpu.make_async_remote_copy(
-            src_ref=coeffs,
-            dst_ref=slab.at[me_a],
-            send_sem=ag_send.at[k],
-            recv_sem=ag_recv.at[k],
-            device_id=(lax.rem(me_a + k, na), me_b),
-            device_id_type=MESH,
-        )
-        copy.start()
-        gathers.append(copy)
-
-    for i in range(5):
+    for i in range(1, 6):
         loads[i].wait()
     pair_ids = lax.broadcasted_iota(jnp.int32, (wide, slots), 0)
     string_ids = lax.broadcasted_iota(jnp.int32, (alphas, slots), 0)
@@ -157,61 +145,88 @@
     g = g_v[...] + jnp.where(own, h, 0.0)
 
     full, rem = slots // LANES, slots % LANES
-    loads[5].wait()
-    bits = cols.bit_length() - 1
-
-    def to_rows(ref, values):
-        for i in range(full):
-            ref[i * cols : (i + 1) * cols, :] = values[i]
-        if rem:
-            ref[full * cols : full * cols + rem, :] = values[full].T[:rem, :]
-
-    def chunks(ref):
-        parts = [ref[:, i * LANES : (i + 1) * LANES] for i in range(full)]
-        if rem:
-            last = ref[:, full * LANES :]
-            parts.append(jnp.concatenate([last, jnp.zeros((cols, LANES - rem), last.dtype)], axis=1))
-        return parts
-
-    targets = [t.astype(f32) for t in chunks(bt_v)]
-    targets = [jnp.floor(t * (1.0 / cols)) for t in targets], targets
-    to_rows(owner_v, targets[0])
-    to_rows(lo_v, [t - o * cols for o, t in zip(*targets)])
-    lo_ids = lax.broadcasted_iota(jnp.int32, (cols, LANES), 0).astype(f32)
+    for i in range(6, 9):
+        loads[i].wait()
+    pair_bits = (wide - 1).bit_length()
+    column_bits = (cols - 1).bit_length()
+
+    def swap(pair):
+        row = (pair * mul) >> shift
+        return (pair - row * norb) * norb + row
+
+    def pack(lower, upper):
+        swapped = swap(bp_v[lower:upper, :])
+        return (bt_v[lower:upper, :] << (pair_bits + 2)) | (swapped << 2) | (bs_v[lower:upper, :] + 1)
+
+    codes = [pack(i * LANES, (i + 1) * LANES).astype(f32).T.astype(jnp.int32) for i in range(full)]
+    for i, code in enumerate(codes):
+        target = code >> (pair_bits + 2)
+        owner_v[i * cols : (i + 1) * cols, :] = (target >> column_bits).astype(f32)
+        lo_v[i * cols : (i + 1) * cols, :] = (target & (cols - 1)).astype(f32)
+    if rem:
+        target = bt_v[full * LANES :, :]
+        owner_v[full * cols : full * cols + rem, :] = (target >> column_bits).astype(f32)
+        lo_v[full * cols : full * cols + rem, :] = (target & (cols - 1)).astype(f32)
+        tail = pack(full * LANES, slots).astype(f32)
+        tail = jnp.concatenate([tail] * rows + [jnp.zeros((LANES - rows * rem, cols), f32)], axis=0)
+        codes.append(tail.T.astype(jnp.int32))
+    swapped = [(code >> 2) & ((1 << pair_bits) - 1) for code in codes]
+    signs = [((code & 3) - 1).astype(f32) for code in codes]
+    lanes = [index & (LANES - 1) for index in swapped]
+    pieces = [index >> (LANES.bit_length() - 1) for index in swapped]
+
+    loads[0].wait()
+    pl.semaphore_wait(barrier, na + nb - 2)
+
+    gathers = []
+    for k in range(1, na):
+        copy = pltpu.make_async_remote_copy(
+            src_ref=c_v,
+            dst_ref=slab.at[me_a],
+            send_sem=ag_send.at[k - 1],
+            recv_sem=ag_recv.at[k - 1],
+            device_id=(lax.rem(me_a + k, na), me_b),
+            device_id_type=MESH,
+        )
+        copy.start()
+        gathers.append(copy)
+
+    lo_ids = lax.broadcasted_iota(jnp.int32, (cols, LANES), 0).astype(f32).astype(bf16)
     items = slots * cols // LANES
 
-    @pl.loop(0, items // step_rows)
+    @pl.loop(0, items // build_rows)
     def _(i):
-        for r in range(step_rows):
-            row = i * step_rows + r
-            match = lo_ids == lo_v[pl.ds(row, 1), :]
-            hot[:, pl.ds(pl.multiple_of(row * LANES, LANES), LANES)] = jnp.where(match, 1.0, 0.0).astype(bf16)
-
-    loads[6].wait()
-    loads[7].wait()
-    lanes, pieces, signs = [], [], []
-    for p, s in zip(chunks(bp_v), chunks(bs_v)):
-        k = (p * mul) >> shift
-        swapped = (p - k * norb) * norb + k
-        lanes.append(swapped & (LANES - 1))
-        pieces.append(swapped >> (LANES.bit_length() - 1))
-        signs.append(s.astype(f32))
+        for r in range(build_rows):
+            row = i * build_rows + r
+            wanted = jnp.broadcast_to(lo_v[pl.ds(row, 1), :].astype(bf16), (cols, LANES))
+            match = jnp.where(lo_ids == wanted, jnp.ones((), bf16), jnp.zeros((), bf16))
+            hot[:, pl.ds(pl.multiple_of(row * LANES, LANES), LANES)] = match
 
     for copy in gathers:
         copy.wait()
-    slab[me_a] = coeffs[...]
+    slab[me_a] = c_v[...]
     c = jnp.concatenate([slab[i] for i in range(na)], axis=0)
     c_top, c_rest = split(c)
     lhs = jnp.concatenate([c_top, c_rest, c_top], axis=0).T.astype(bf16)
-    local = []
+    local, focks = [], []
     for a in range(rows):
         local.append(jnp.sum(weight[a * alphas : (a + 1) * alphas] * c, axis=0, keepdims=True))
         g_top, g_rest = split(g[a * alphas : (a + 1) * alphas])
-        fock = dot(lhs, jnp.concatenate([g_top, g_top, g_rest], axis=0).astype(bf16))
-        picked = [lane_pick(fock, l, p) * s for l, p, s in zip(lanes, pieces, signs)]
-        parts = [split(v) for v in picked]
-        to_rows(vals.at[a], [v[0] for v in parts])
-        to_rows(vals.at[rows + a], [v[1] for v in parts])
+        focks.append(dot(lhs, jnp.concatenate([g_top, g_top, g_rest], axis=0).astype(bf16)))
+    for i in range(full):
+        for a in range(rows):
+            top, rest = split(lane_pick(focks[a], lanes[i], pieces[i]) * signs[i])
+            vals[a, i * cols : (i + 1) * cols, :] = top
+            vals[rows + a, i * cols : (i + 1) * cols, :] = rest
+    if rem:
+        lane_ids = lax.broadcasted_iota(jnp.int32, (cols, LANES), 1)
+        tail = lane_pick(focks[0], lanes[full], pieces[full])
+        for a in range(1, rows):
+            tail = jnp.where(lane_ids < a * rem, tail, lane_pick(focks[a], lanes[full], pieces[full]))
+        top, rest = split((tail * signs[full]).T)
+        for a in range(rows):
+            vals[a, full * cols : full * cols + rem, :] = top[a * rem : (a + 1) * rem]
+            vals[rows + a, full * cols : full * cols + rem, :] = rest[a * rem : (a + 1) * rem]
 
     owner_ids = lax.broadcasted_iota(jnp.int32, (nb, LANES), 0).astype(f32)
 
@@ -236,9 +251,9 @@
         to = lax.rem(me_b + k, nb)
         copy = pltpu.make_async_remote_copy(
             src_ref=send.at[to],
-            dst_ref=recv.at[k],
-            send_sem=rs_send.at[k],
-            recv_sem=rs_recv.at[k],
+            dst_ref=recv.at[k - 1],
+            send_sem=rs_send.at[k - 1],
+            recv_sem=rs_recv.at[k - 1],
             device_id=(me_a, to),
             device_id_type=MESH,
         )
@@ -248,7 +263,7 @@
     for copy in copies:
         copy.wait()
     for k in range(1, nb):
-        result = result + recv[k]
+        result = result + recv[k - 1]
     out[...] = result
 
 
@@ -261,21 +276,23 @@
         norb = one_body.shape[0]
         wide = pl.cdiv(norb * norb, LANES) * LANES
         items = slots * cols // LANES
-        step_rows = next(n for n in (6, 4, 3, 2, 1) if items % n == 0)
+        build_rows = next(n for n in range(12, 0, -1) if items % n == 0)
+        step_rows = next(n for n in range(24, 0, -1) if items % n == 0)
         i32, f32 = jnp.int32, jnp.float32
         padded = pl.cdiv(items, 8) * 8
         return pl.pallas_call(
-            functools.partial(kernel, na, nb, step_rows),
+            functools.partial(kernel, na, nb, build_rows, step_rows),
             out_shape=jax.ShapeDtypeStruct((rows, cols), f32),
-            in_specs=[pl.BlockSpec(memory_space=pltpu.VMEM)] + [pl.BlockSpec(memory_space=pl.ANY)] * 8,
+            in_specs=[pl.BlockSpec(memory_space=pl.ANY)] * 9,
             out_specs=pl.BlockSpec(memory_space=pltpu.VMEM),
             scratch_shapes=[
+                pltpu.VMEM(coeffs.shape, f32),
                 pltpu.VMEM(a_target.shape, i32),
                 pltpu.VMEM(a_pair.shape, i32),
                 pltpu.VMEM(a_sign.shape, i32),
-                pltpu.VMEM(b_target.shape, i32),
-                pltpu.VMEM(b_pair.shape, i32),
-                pltpu.VMEM(b_sign.shape, i32),
+                pltpu.VMEM(b_target.shape[::-1], i32),
+                pltpu.VMEM(b_pair.shape[::-1], i32),
+                pltpu.VMEM(b_sign.shape[::-1], i32),
                 pltpu.VMEM(integrals.shape, f32),
                 pltpu.VMEM(one_body.shape, f32),
                 pltpu.VMEM((na, rows, cols), f32),
@@ -285,15 +302,15 @@
                 pltpu.VMEM((2 * rows, padded, LANES), f32),
                 pltpu.VMEM((cols, items * LANES), jnp.bfloat16),
                 pltpu.VMEM((nb, rows, cols), f32),
-                pltpu.VMEM((nb, rows, cols), f32),
-                pltpu.SemaphoreType.DMA((8,)),
-                pltpu.SemaphoreType.DMA((na,)),
-                pltpu.SemaphoreType.DMA((na,)),
-                pltpu.SemaphoreType.DMA((nb,)),
-                pltpu.SemaphoreType.DMA((nb,)),
+                pltpu.VMEM((nb - 1, rows, cols), f32),
+                pltpu.SemaphoreType.DMA((9,)),
+                pltpu.SemaphoreType.DMA((na - 1,)),
+                pltpu.SemaphoreType.DMA((na - 1,)),
+                pltpu.SemaphoreType.DMA((nb - 1,)),
+                pltpu.SemaphoreType.DMA((nb - 1,)),
             ],
             compiler_params=pltpu.CompilerParams(collective_id=0, has_side_effects=True),
-        )(coeffs, a_target, a_pair, a_sign, b_target, b_pair, b_sign, integrals, one_body)
+        )(coeffs, a_target, a_pair, a_sign, b_target.T, b_pair.T, b_sign.T, integrals, one_body)
 
     placed = (
         P("alpha", "beta"),

time: 22.9 us -> 18 us (0.79)
  local copies, waits for them, and re-layouts: 4.53 us -> 1.24 us
  Pallas kernels: 18.1 us -> 16.6 us
    unnamed x8 -> x1, local copies, waits for them, and re-layouts: 4.53 us -> 1.24 us
    pallas_call x1, Pallas kernels: 18.1 us -> 16.6 us  [per_device(): pl.pallas_call(functools.partial(kernel, na, nb, build_rows, step_rows),...]
where the time goes in v2:
time: 18 us; the launch traced here: 17.9 us
  Pallas kernels  16.6 us (92%)
  local copies, waits for them, and re-layouts  1.24 us (7%)
    pallas_call x1, Pallas kernels, per_device(): pl.pallas_call(functools.partial(kernel, na, nb, build_rows, step_rows),...  16.6 us
    unnamed x1, local copies, waits for them, and re-layouts  1.24 us

profile of v2, /device:TPU:0, one launch (start us, length us, event | category | flops | bytes accessed | tf_op | source)
XLA Modules:
  0.0 17.9 jit_solution(10017596882542157669)
XLA Ops:
  0.0 16.6 %shard_map.91 = f32[2,128]{1,0:T(2,128)} custom-call(f32[2,128]{1,0:T(2,128)} %coeffs.1, s32[2,132]{1,0:T(2,128)} %a_target.1, s32[2,132]{1,0:T(2,128)} %a_pair.1, s32[2,132]{1,0:T(2,128)} %a_sign.1, s32[132,128]{1,0:T(8,128)} %bitcast.3, s32[132,128]{1,0:T(8,128)} %bitcast.4, s32[132,128]{1,0:T(8,128)} %bitcast.5, f32[484,484]{1,0:T(8,128)} %integrals.1, ...), custom_call_target="tpu_custom_call" | custom-call | tf_op jit(solution)/shard_map/pallas_call | solution.py:283
  16.6 1.2 %copy.11 = f32[2,128]{1,0:T(2,128)} copy(f32[2,128]{1,0:T(2,128)} %shard_map.91) | data formatting | bytes 2048

commit v3 on v2

--- a/solution.py
+++ b/solution.py
@@ -110,6 +110,22 @@
         pl.semaphore_signal(barrier, inc=1, device_id=(lax.rem(me_a + k, na), me_b), device_id_type=MESH)
     for k in range(1, nb):
         pl.semaphore_signal(barrier, inc=1, device_id=(me_a, lax.rem(me_b + k, nb)), device_id_type=MESH)
+    loads[0].wait()
+    pl.semaphore_wait(barrier, na + nb - 2)
+
+    gathers = []
+    for k in range(1, na):
+        copy = pltpu.make_async_remote_copy(
+            src_ref=c_v,
+            dst_ref=slab.at[me_a],
+            send_sem=ag_send.at[k - 1],
+            recv_sem=ag_recv.at[k - 1],
+            device_id=(lax.rem(me_a + k, na), me_b),
+            device_id_type=MESH,
+        )
+        copy.start()
+        gathers.append(copy)
+
     for i in range(1, 6):
         loads[i].wait()
     pair_ids = lax.broadcasted_iota(jnp.int32, (wide, slots), 0)
@@ -174,22 +190,6 @@
     signs = [((code & 3) - 1).astype(f32) for code in codes]
     lanes = [index & (LANES - 1) for index in swapped]
     pieces = [index >> (LANES.bit_length() - 1) for index in swapped]
-
-    loads[0].wait()
-    pl.semaphore_wait(barrier, na + nb - 2)
-
-    gathers = []
-    for k in range(1, na):
-        copy = pltpu.make_async_remote_copy(
-            src_ref=c_v,
-            dst_ref=slab.at[me_a],
-            send_sem=ag_send.at[k - 1],
-            recv_sem=ag_recv.at[k - 1],
-            device_id=(lax.rem(me_a + k, na), me_b),
-            device_id_type=MESH,
-        )
-        copy.start()
-        gathers.append(copy)
 
     lo_ids = lax.broadcasted_iota(jnp.int32, (cols, LANES), 0).astype(f32).astype(bf16)
     items = slots * cols // LANES

time: 18 us -> 16.8 us (0.933)
  Pallas kernels: 16.6 us -> 15.4 us
    pallas_call x1, Pallas kernels: 16.6 us -> 15.4 us  [per_device(): pl.pallas_call(functools.partial(kernel, na, nb, build_rows, step_rows),...]
where the time goes in v3:
time: 16.8 us; the launch traced here: 16.6 us
  Pallas kernels  15.4 us (92%)
  local copies, waits for them, and re-layouts  1.24 us (7%)
    pallas_call x1, Pallas kernels, per_device(): pl.pallas_call(functools.partial(kernel, na, nb, build_rows, step_rows),...  15.4 us
    unnamed x1, local copies, waits for them, and re-layouts  1.24 us

profile of v3, /device:TPU:0, one launch (start us, length us, event | category | flops | bytes accessed | tf_op | source)
XLA Modules:
  0.0 16.6 jit_solution(2572765259013706923)
XLA Ops:
  0.0 15.4 %shard_map.91 = f32[2,128]{1,0:T(2,128)} custom-call(f32[2,128]{1,0:T(2,128)} %coeffs.1, s32[2,132]{1,0:T(2,128)} %a_target.1, s32[2,132]{1,0:T(2,128)} %a_pair.1, s32[2,132]{1,0:T(2,128)} %a_sign.1, s32[132,128]{1,0:T(8,128)} %bitcast.3, s32[132,128]{1,0:T(8,128)} %bitcast.4, s32[132,128]{1,0:T(8,128)} %bitcast.5, f32[484,484]{1,0:T(8,128)} %integrals.1, ...), custom_call_target="tpu_custom_call" | custom-call | tf_op jit(solution)/shard_map/pallas_call | solution.py:283
  15.4 1.2 %copy.11 = f32[2,128]{1,0:T(2,128)} copy(f32[2,128]{1,0:T(2,128)} %shard_map.91) | data formatting | bytes 2048

commit v4 on v3

--- a/solution.py
+++ b/solution.py
@@ -240,9 +240,12 @@
             )
         lhs = jnp.concatenate(lhs, axis=1).astype(bf16)
         width = step_rows * LANES
-        return total + dot(lhs, hot[:, pl.ds(pl.multiple_of(i * width, LANES), width)], NT)
-
-    total = lax.fori_loop(0, items // step_rows, step, jnp.zeros((2 * rows * nb, cols), f32))
+        return total + dot(hot[:, pl.ds(pl.multiple_of(i * width, LANES), width)], lhs, NT)
+
+    total = lax.fori_loop(0, items // step_rows, step, jnp.zeros((cols, 2 * rows * nb), f32))
+    if total.shape[1] % LANES:
+        total = jnp.concatenate([total, jnp.zeros((cols, -total.shape[1] % LANES), f32)], axis=1)
+    total = total.T
     for a in range(rows):
         send[:, a, :] = total[a * nb : (a + 1) * nb] + total[(rows + a) * nb : (rows + a + 1) * nb]
 
@@ -277,7 +280,7 @@
         wide = pl.cdiv(norb * norb, LANES) * LANES
         items = slots * cols // LANES
         build_rows = next(n for n in range(12, 0, -1) if items % n == 0)
-        step_rows = next(n for n in range(24, 0, -1) if items % n == 0)
+        step_rows = items
         i32, f32 = jnp.int32, jnp.float32
         padded = pl.cdiv(items, 8) * 8
         return pl.pallas_call(

time: 16.8 us -> 15.5 us (0.923)
  Pallas kernels: 15.4 us -> 14.1 us
    pallas_call x1, Pallas kernels: 15.4 us -> 14.1 us  [per_device(): pl.pallas_call(functools.partial(kernel, na, nb, build_rows, step_rows),...]
where the time goes in v4:
time: 15.5 us; the launch traced here: 15.3 us
  Pallas kernels  14.1 us (91%)
  local copies, waits for them, and re-layouts  1.24 us (8%)
    pallas_call x1, Pallas kernels, per_device(): pl.pallas_call(functools.partial(kernel, na, nb, build_rows, step_rows),...  14.1 us
    unnamed x1, local copies, waits for them, and re-layouts  1.24 us

profile of v4, /device:TPU:0, one launch (start us, length us, event | category | flops | bytes accessed | tf_op | source)
XLA Modules:
  0.0 15.3 jit_solution(10080195180241299231)
XLA Ops:
  0.0 14.1 %shard_map.91 = f32[2,128]{1,0:T(2,128)} custom-call(f32[2,128]{1,0:T(2,128)} %coeffs.1, s32[2,132]{1,0:T(2,128)} %a_target.1, s32[2,132]{1,0:T(2,128)} %a_pair.1, s32[2,132]{1,0:T(2,128)} %a_sign.1, s32[132,128]{1,0:T(8,128)} %bitcast.3, s32[132,128]{1,0:T(8,128)} %bitcast.4, s32[132,128]{1,0:T(8,128)} %bitcast.5, f32[484,484]{1,0:T(8,128)} %integrals.1, ...), custom_call_target="tpu_custom_call" | custom-call | tf_op jit(solution)/shard_map/pallas_call | solution.py:286
  14.1 1.2 %copy.11 = f32[2,128]{1,0:T(2,128)} copy(f32[2,128]{1,0:T(2,128)} %shard_map.91) | data formatting | bytes 2048

commit v5 on v4

--- a/solution.py
+++ b/solution.py
@@ -213,11 +213,6 @@
         local.append(jnp.sum(weight[a * alphas : (a + 1) * alphas] * c, axis=0, keepdims=True))
         g_top, g_rest = split(g[a * alphas : (a + 1) * alphas])
         focks.append(dot(lhs, jnp.concatenate([g_top, g_top, g_rest], axis=0).astype(bf16)))
-    for i in range(full):
-        for a in range(rows):
-            top, rest = split(lane_pick(focks[a], lanes[i], pieces[i]) * signs[i])
-            vals[a, i * cols : (i + 1) * cols, :] = top
-            vals[rows + a, i * cols : (i + 1) * cols, :] = rest
     if rem:
         lane_ids = lax.broadcasted_iota(jnp.int32, (cols, LANES), 1)
         tail = lane_pick(focks[0], lanes[full], pieces[full])
@@ -228,6 +223,11 @@
             vals[a, full * cols : full * cols + rem, :] = top[a * rem : (a + 1) * rem]
             vals[rows + a, full * cols : full * cols + rem, :] = rest[a * rem : (a + 1) * rem]
 
+    for i in range(full):
+        for a in range(rows):
+            top, rest = split(lane_pick(focks[a], lanes[i], pieces[i]) * signs[i])
+            vals[a, i * cols : (i + 1) * cols, :] = top
+            vals[rows + a, i * cols : (i + 1) * cols, :] = rest
     owner_ids = lax.broadcasted_iota(jnp.int32, (nb, LANES), 0).astype(f32)
 
     def step(i, total):
@@ -279,7 +279,7 @@
         norb = one_body.shape[0]
         wide = pl.cdiv(norb * norb, LANES) * LANES
         items = slots * cols // LANES
-        build_rows = next(n for n in range(12, 0, -1) if items % n == 0)
+        build_rows = next(n for n in range(44, 0, -1) if items % n == 0)
         step_rows = items
         i32, f32 = jnp.int32, jnp.float32
         padded = pl.cdiv(items, 8) * 8

time: 15.5 us -> 15.5 us (level)
  no operation moved by 1% of the time
where the time goes in v5:
time: 15.5 us; the launch traced here: 15.3 us
  Pallas kernels  14.1 us (91%)
  local copies, waits for them, and re-layouts  1.24 us (8%)
    pallas_call x1, Pallas kernels, per_device(): pl.pallas_call(functools.partial(kernel, na, nb, build_rows, step_rows),...  14.1 us
    unnamed x1, local copies, waits for them, and re-layouts  1.24 us

profile of v5, /device:TPU:0, one launch (start us, length us, event | category | flops | bytes accessed | tf_op | source)
XLA Modules:
  0.0 15.3 jit_solution(11739400306748607067)
XLA Ops:
  0.0 14.1 %shard_map.91 = f32[2,128]{1,0:T(2,128)} custom-call(f32[2,128]{1,0:T(2,128)} %coeffs.1, s32[2,132]{1,0:T(2,128)} %a_target.1, s32[2,132]{1,0:T(2,128)} %a_pair.1, s32[2,132]{1,0:T(2,128)} %a_sign.1, s32[132,128]{1,0:T(8,128)} %bitcast.3, s32[132,128]{1,0:T(8,128)} %bitcast.4, s32[132,128]{1,0:T(8,128)} %bitcast.5, f32[484,484]{1,0:T(8,128)} %integrals.1, ...), custom_call_target="tpu_custom_call" | custom-call | tf_op jit(solution)/shard_map/pallas_call | solution.py:286
  14.1 1.2 %copy.11 = f32[2,128]{1,0:T(2,128)} copy(f32[2,128]{1,0:T(2,128)} %shard_map.91) | data formatting | bytes 2048
